TPU v7x, 256 devices: a whole 4x4x8 slice. The times are simulated.
256 devices in a mesh: src: 16 (over z_lo, y), rcv: 16 (over z_hi, x, core).
Axes of the slice: x: 4, y: 4, z: 8 (z_hi: 2, z_lo: 4; z = z_hi * 4 + z_lo), core: 2. Of those that a mesh axis runs over, the one named last changes fastest.
Arguments:
- records: bfloat16 [4096, 8192], P(('rcv', 'src')), may hold values from -6 to 6
- live_mask: int32 [4096], P(('rcv', 'src')), may hold values 0 or 1
- offsets: int32 [64], replicated, may hold values from 0 to 7936
- block_ids: int32 [2, 16], P(None, 'src'), may hold values from 0 to 31
Outputs:
- stacked: bfloat16 [2, 76, 2048, 4096], P(None, None, 'src', 'rcv')
All inputs are finite; a program needn't handle non-finite values. No bound on the sum of `live_mask` on one device may be relied on, other than what follows from the above.
Results may differ from a plain program's by a relative error of at most 0.0059.
Values may be sent and summed in bfloat16 or wider, within the bound.
A program may use at most 128 MiB of HBM per device.

v0:
```python
import jax
import jax.numpy as jnp
from jax import lax
from jax.sharding import PartitionSpec as P

L = 256
SB = 128
LAGS = 76


def broadcast(value, axis, source):
    kept = jnp.where(lax.axis_index(axis) == source, value, 0).astype(value.dtype)
    return lax.psum(kept, axis)


def build_tables(length, win_count, lag_count):
    sample_axis = jnp.arange(length, dtype=jnp.float32)
    bin_count = length // 2
    bin_axis = jnp.arange(bin_count, dtype=jnp.float32)
    phases = 2.0 * jnp.pi * sample_axis[:, None] * bin_axis[None, :] / length
    taper = 0.5 - 0.5 * jnp.cos(2.0 * jnp.pi * sample_axis / length)
    dft_table = jnp.concatenate(
        [taper[:, None] * jnp.cos(phases), -taper[:, None] * jnp.sin(phases)], axis=1
    ).astype(jnp.bfloat16)
    lag_axis = jnp.arange(lag_count, dtype=jnp.float32)
    weights = jnp.where(bin_axis == 0, 1.0, 2.0).astype(jnp.float32)
    lag_table = (
        weights[:, None]
        * jnp.cos(2.0 * jnp.pi * bin_axis[:, None] * lag_axis[None, :] / length)
        * (2.0 / (win_count * length))
    ).astype(jnp.bfloat16)
    return (dft_table, lag_table)


def transform(live_rec, offsets, dft_table):
    receiver_total = live_rec.shape[0]
    length = dft_table.shape[0]
    win_count = offsets.shape[0]
    windows = jax.vmap(lambda anchor: lax.dynamic_slice_in_dim(live_rec, anchor, length, 1))(
        offsets
    )
    flat_spec = jnp.dot(
        windows.reshape(win_count * receiver_total, length),
        dft_table,
        preferred_element_type=jnp.float32,
    ).astype(jnp.bfloat16)
    bin_count = dft_table.shape[1] // 2
    return (
        flat_spec.reshape(win_count, receiver_total, 2, bin_count)
        .transpose(3, 1, 2, 0)
        .reshape(bin_count, receiver_total, 2 * win_count)
    )


def correlate(source_block, receiver_block, lag_table, src_chan, rcv_chan):
    cross_spectrum = jnp.einsum(
        "mdt,mpt->mdp", source_block, receiver_block, preferred_element_type=jnp.float32
    ).astype(jnp.bfloat16)
    bin_count, src_count, receiver_total = cross_spectrum.shape
    mixed = jnp.dot(
        lag_table.T,
        cross_spectrum.reshape(bin_count, src_count * receiver_total),
        preferred_element_type=jnp.float32,
    )
    mixed = mixed.reshape(-1, src_count, receiver_total)
    self_pair = src_chan[:, None] == rcv_chan[None, :]
    return jnp.where(self_pair[None], 0.0, mixed).astype(jnp.bfloat16)


def local(records, live_mask, offsets, block_ids):
    group_member_count = records.shape[0] * lax.axis_size("src")
    dft_table, lag_table = build_tables(L, offsets.shape[0], LAGS)
    live_rec = records * live_mask[:, None].astype(records.dtype)
    local_spectrum = transform(live_rec, offsets, dft_table)
    receiver_block = lax.all_gather(local_spectrum, "src", axis=1, tiled=True)
    rcv_chan = lax.axis_index("rcv") * group_member_count + jnp.arange(
        group_member_count, dtype=jnp.int32
    )
    results = []
    for turn_index in range(block_ids.shape[0]):
        block_id = block_ids[turn_index, 0]
        first_chan = block_id * SB
        root_rank = first_chan // group_member_count
        beginning = first_chan % group_member_count
        portion = lax.dynamic_slice_in_dim(receiver_block, beginning, SB, 1)
        source_block = broadcast(portion, "rcv", root_rank)
        src_chan = first_chan + jnp.arange(SB, dtype=jnp.int32)
        results.append(correlate(source_block, receiver_block, lag_table, src_chan, rcv_chan))
    return jnp.stack(results)


def solution(mesh):
    in_specs = (P(("rcv", "src"), None), P(("rcv", "src")), P(), P(None, "src"))
    out_specs = P(None, None, "src", "rcv")
    return jax.shard_map(local, mesh=mesh, in_specs=in_specs, out_specs=out_specs, check_vma=False)
```

profile of v0, /device:TPU:32, one launch (start us, length us, event | category | flops | bytes accessed | tf_op | source)
XLA Modules:
  0.0 583.0 jit_solution(16682871106229429336)
XLA Ops:
  8.0 1.0 broadcast_multiply_fusion
  9.0 85.5 %while.1 = (s32[]{:T(128)}, bf16[16,8192]{1,0:T(8,128)(2,1)S(1)}, s32[64,2]{0,1:T(2,128)S(1)}, bf16[64,16,256]{2,1,0:T(8,128)(2,1)S(1)}, s32[]{:T(128)}) while((s32[]{:T(128)}, bf16[16,8192]{1,0:T(8,128)(2,1)S(1)}, s32[64,2]{0,1:T(2,128)S(1)}, bf16[64,16,256]{2,1,0:T(8,128)(2,1)S(1)}, s32[]{:T(128)}) %tuple.23), condition=%wide.while_cond, body=%wide.while_body.sunk | while | flops 2 | bytes 16481 | solution.py:39
  9.7 0.7 bitcast_dynamic-update-slice_fusion.2
  11.0 0.7 bitcast_dynamic-update-slice_fusion.2
  13.7 0.7 bitcast_dynamic-update-slice_fusion.2
  15.0 0.7 bitcast_dynamic-update-slice_fusion.2
  16.3 0.7 bitcast_dynamic-update-slice_fusion.2
  17.7 0.7 bitcast_dynamic-update-slice_fusion.2
  19.0 0.7 bitcast_dynamic-update-slice_fusion.2
  95.8 1.2 copy.10
  97.1 1.3 fusion.21
  99.6 125.3 %all-gather.2.cloned.1.call-done = bf16[128,256,128]{2,1,0:T(8,128)(2,1)} async-done(((bf16[128,16,128]{2,1,0:T(8,128)(2,1)}), bf16[128,256,128]{2,1,0:T(8,128)(2,1)}) %all-gather.2.cloned.1.call-update) | async-done | bytes 8388624 | tf_op jit(solution)/shard_map/all_gather | solution.py:75
  224.9 11.2 %dynamic-slice_select_fusion.1 = (bf16[128,128,128]{2,1,0:T(8,128)(2,1)}, bf16[128,128,128]{2,1,0:T(8,128)(2,1)}) fusion(bf16[128,256,128]{2,1,0:T(8,128)(2,1)} %all-gather.2.cloned.1.call-done, s32[]{:T(128)S(6)} %select_n.63, pred[]{:T(512)S(6)} %eq.58, s32[]{:T(128)S(6)} %select_n.69, pred[]{:T(512)S(6)} %eq.61), kind=kLoop, calls=%fused_computation.10 | loop fusion | flops 4194304 | bytes 16777226 | tf_op jit(solution)/shard_map/jit(_where)/select_n | solution.py:12
  236.3 235.9 %all-reduce.4.cloned.1.call-done = (bf16[128,128,128]{2,1,0:T(8,128)(2,1)}, bf16[128,128,128]{2,1,0:T(8,128)(2,1)}) async-done(((bf16[128,128,128]{2,1,0:T(8,128)(2,1)}, bf16[128,128,128]{2,1,0:T(8,128)(2,1)}), (bf16[128,128,128]{2,1,0:T(8,128)(2,1)}, bf16[128,128,128]{2,1,0:T(8,128)(2,1)})) %all-reduce.4.cloned.1.call-update) | async-done | bytes 8388624 | tf_op jit(solution)/shard_map/psum | solution.py:13
  472.2 10.4 %convolution_convert_fusion.1 = bf16[128,128,256]{2,1,0:T(8,128)(2,1)} fusion(bf16[128,128,128]{2,1,0:T(8,128)(2,1)} %get-tuple-element.22, bf16[128,256,128]{2,1,0:T(8,128)(2,1)} %all-gather.2.cloned.1.call-done), kind=kOutput, calls=%fused_computation.6 | convolution fusion | flops 1077936128 | bytes 20971520 | tf_op jit(solution)/shard_map/mdt,mpt->mdp/dot_general | solution.py:56
  482.6 12.5 %copy.14 = bf16[16,8,128,256]{3,1,2,0:T(8,128)(2,1)} copy(bf16[16,8,128,256]{3,2,1,0:T(8,128)(2,1)} %bitcast.43) | data formatting | bytes 16777216
  495.1 11.3 %copy.11 = bf16[32768,128]{1,0:T(8,128)(2,1)} copy(bf16[32768,128]{0,1:T(8,128)(2,1)} %bitcast.44) | data formatting | bytes 16777216 | tf_op jit(solution)/shard_map/dot_general | solution.py:60
  506.4 10.4 %convolution_convert_fusion = bf16[128,128,256]{2,1,0:T(8,128)(2,1)} fusion(bf16[128,128,128]{2,1,0:T(8,128)(2,1)} %get-tuple-element.21, bf16[128,256,128]{2,1,0:T(8,128)(2,1)} %all-gather.2.cloned.1.call-done), kind=kOutput, calls=%fused_computation.5 | convolution fusion | flops 1077936128 | bytes 20971520 | tf_op jit(solution)/shard_map/mdt,mpt->mdp/dot_general | solution.py:56
  516.8 12.3 %copy.15 = bf16[16,8,128,256]{3,1,2,0:T(8,128)(2,1)} copy(bf16[16,8,128,256]{3,2,1,0:T(8,128)(2,1)} %bitcast.42) | data formatting | bytes 16777216
  529.2 11.9 %copy.12 = bf16[32768,128]{1,0:T(8,128)(2,1)} copy(bf16[32768,128]{0,1:T(8,128)(2,1)} %bitcast.45) | data formatting | bytes 16777216 | tf_op jit(solution)/shard_map/dot_general | solution.py:60
  541.1 9.0 %fusion = bf16[1,76,128,256]{3,1,2,0:T(8,128)(2,1)} fusion(pred[128,256]{1,0:T(8,128)(4,1)S(1)} %get-tuple-element.25, bf16[128,256,128]{2,1,0:T(8,128)(2,1)} %bitcast.40, f32[128]{0:T(128)S(1)} %get-tuple-element.36, f32[128]{0:T(128)S(1)} %get-tuple-element.35), kind=kOutput, calls=%fused_computation.7 | convolution fusion | flops 642563584 | bytes 13403136 | tf_op jit(solution)/shard_map/dot_general | solution.py:60
  550.0 5.5 fusion.1
  555.5 9.0 %pad_maximum_fusion = bf16[2,76,128,256]{3,1,2,0:T(8,128)(2,1)} fusion(bf16[1,76,128,256]{3,1,2,0:T(8,128)(2,1)} %fusion.1, bf16[1,76,128,256]{3,1,2,0:T(8,128)(2,1)} %fusion), kind=kLoop, calls=%fused_computation.2 | loop fusion | flops 4980736 | bytes 19922944 | tf_op jit(solution)/shard_map/stack | solution.py:89
  564.5 11.6 %copy.13 = bf16[2,76,128,256]{3,2,1,0:T(8,128)(2,1)} copy(bf16[2,76,128,256]{3,1,2,0:T(8,128)(2,1)} %pad_maximum_fusion) | data formatting | bytes 19922944 | tf_op jit(solution)/shard_map/stack | solution.py:89
  (205 shorter events, 83.3 us)
Async XLA Ops:
  6.5 218.3 %all-gather.2.cloned.1.call-start = ((), (), s32[]{:S(2)}) async-start(), calls=%async_computation | async-start | bytes 8912896 | tf_op jit(solution)/shard_map/all_gather | solution.py:75
  97.0 375.2 %all-reduce.4.cloned.1.call-start = ((), (), s32[]{:S(2)}) async-start(), calls=%async_computation.1 | async-start | bytes 16777216 | tf_op jit(solution)/shard_map/psum | solution.py:13
  541.1 9.0 %copy-start = (bf16[32768,128]{1,0:T(8,128)(2,1)S(1)}, bf16[32768,128]{1,0:T(8,128)(2,1)}, u32[]{:S(2)}) copy-start(bf16[32768,128]{1,0:T(8,128)(2,1)} %copy.12) | copy-start | bytes 25165828
Sparse Core Ops, SparseCore 0:
  97.1 127.7 all-gather.1
  236.3 235.8 all-reduce.3
where the time goes:
time: 584 us; the launch traced here: 583 us
  waiting for transfers between devices  361 us (62%)
  local copies, waits for them, and re-layouts  148 us (25%)
  matrix products  35.6 us (6%)
  other arithmetic  23.4 us (4%)
  between operations  14.7 us (3%)
    psum x1, waiting for transfers between devices, broadcast(): return lax.psum(kept, axis)  236 us
    all_gather x1, waiting for transfers between devices, local(): receiver_block = lax.all_gather(local_spectrum, 'src', axis=1, tiled=True)  125 us
    gather x192, local copies, waits for them, and re-layouts  85.4 us
    unnamed x4, local copies, waits for them, and re-layouts  24.9 us
    dot_general x2, local copies, waits for them, and re-layouts, correlate(): jnp.dot(lag_table.T, cross_spectrum.reshape(bin_count, src_count * receiv...  23.2 us
    dot_general x2, matrix products, correlate(): jnp.einsum('mdt,mpt->mdp', source_block, receiver_block, preferred_elemen...  20.8 us
    dot_general x2, matrix products, correlate(): jnp.dot(lag_table.T, cross_spectrum.reshape(bin_count, src_count * receiv...  14.5 us
  transfers between devices with their start and end apart: 2, of which 2 were waited for; matrix products, arithmetic and copies ran while one was open for 0% of the time, Pallas kernels for 0%

commit v1 on v0

--- a/solution.py
+++ b/solution.py
@@ -72,7 +72,9 @@
     dft_table, lag_table = build_tables(L, offsets.shape[0], LAGS)
     live_rec = records * live_mask[:, None].astype(records.dtype)
     local_spectrum = transform(live_rec, offsets, dft_table)
-    receiver_block = lax.all_gather(local_spectrum, "src", axis=1, tiled=True)
+    receiver_block = jnp.concatenate(
+        lax.all_to_all(jnp.stack([local_spectrum] * lax.axis_size("src")), "src", 0, 0), axis=1
+    )
     rcv_chan = lax.axis_index("rcv") * group_member_count + jnp.arange(
         group_member_count, dtype=jnp.int32
     )

time: 584 us -> 665 us (1.14)
  waiting for transfers between devices: 361 us -> 416 us
  local copies, waits for them, and re-layouts: 148 us -> 161 us
  starting transfers between devices: 0.04 us -> 9.06 us
    all_to_all x0 -> x1, waiting for transfers between devices: none -> 178 us  [local(): lax.all_to_all(jnp.stack([local_spectrum] * lax.axis_size('src')), 'src',...]
    all_gather x1 -> x0, waiting for transfers between devices: 125 us -> none  [local(): receiver_block = lax.all_gather(local_spectrum, 'src', axis=1, tiled=True)]
    all_to_all x0 -> x1, starting transfers between devices: none -> 8.77 us  [local(): lax.all_to_all(jnp.stack([local_spectrum] * lax.axis_size('src')), 'src',...]
    reshape x1, local copies, waits for them, and re-layouts: 1.19 us -> 9.25 us  [local(): jnp.concatenate(lax.all_to_all(jnp.stack([local_spectrum] * lax.axis_size...]
    unnamed x4 -> x6, local copies, waits for them, and re-layouts: 24.9 us -> 25.3 us
where the time goes in v1:
time: 665 us; the launch traced here: 660 us
  waiting for transfers between devices  416 us (63%)
  local copies, waits for them, and re-layouts  161 us (24%)
  matrix products  35.3 us (5%)
  other arithmetic  23.3 us (4%)
  between operations  15 us (2%)
  starting transfers between devices  9.06 us (1%)
    psum x1, waiting for transfers between devices, broadcast(): return lax.psum(kept, axis)  239 us
    all_to_all x1, waiting for transfers between devices, local(): lax.all_to_all(jnp.stack([local_spectrum] * lax.axis_size('src')), 'src',...  178 us
    gather x192, local copies, waits for them, and re-layouts  85.4 us
    unnamed x6, local copies, waits for them, and re-layouts  25.3 us
    dot_general x2, local copies, waits for them, and re-layouts, correlate(): jnp.dot(lag_table.T, cross_spectrum.reshape(bin_count, src_count * receiv...  23.4 us
    dot_general x2, matrix products, correlate(): jnp.einsum('mdt,mpt->mdp', source_block, receiver_block, preferred_elemen...  20.5 us
    dot_general x2, matrix products, correlate(): jnp.dot(lag_table.T, cross_spectrum.reshape(bin_count, src_count * receiv...  14.5 us
  transfers between devices with their start and end apart: 2, of which 2 were waited for; matrix products, arithmetic and copies ran while one was open for 0% of the time, Pallas kernels for 0%

profile of v1, /device:TPU:32, one launch (start us, length us, event | category | flops | bytes accessed | tf_op | source)
XLA Modules:
  0.0 660.3 jit_solution(5575050207625884485)
XLA Ops:
  8.0 1.0 broadcast_multiply_fusion
  9.0 85.5 %while.1 = (s32[]{:T(128)}, bf16[16,8192]{1,0:T(8,128)(2,1)S(1)}, s32[64,2]{0,1:T(2,128)S(1)}, bf16[64,16,256]{2,1,0:T(8,128)(2,1)S(1)}, s32[]{:T(128)}) while((s32[]{:T(128)}, bf16[16,8192]{1,0:T(8,128)(2,1)S(1)}, s32[64,2]{0,1:T(2,128)S(1)}, bf16[64,16,256]{2,1,0:T(8,128)(2,1)S(1)}, s32[]{:T(128)}) %tuple.23), condition=%wide.while_cond, body=%wide.while_body.sunk | while | flops 2 | bytes 16481 | solution.py:39
  9.7 0.7 bitcast_dynamic-update-slice_fusion.2
  11.0 0.7 bitcast_dynamic-update-slice_fusion.2
  12.3 0.7 bitcast_dynamic-update-slice_fusion.2
  13.7 0.7 bitcast_dynamic-update-slice_fusion.2
  15.0 0.7 bitcast_dynamic-update-slice_fusion.2
  16.3 0.7 bitcast_dynamic-update-slice_fusion.2
  96.2 5.0 stack.12
  101.2 8.8 %all-to-all-start = ((bf16[16,128,16,128]{3,2,1,0:T(8,128)(2,1)}), bf16[16,128,16,128]{3,2,1,0:T(8,128)(2,1)}, u32[]{:S(2)}, u32[]{:S(2)}) async-start(bf16[16,128,16,128]{3,2,1,0:T(8,128)(2,1)} %stack.12), calls=%async_computation | async-start | bytes 16777216 | tf_op jit(solution)/shard_map/all_to_all | solution.py:76
  112.2 177.6 %all-to-all-done = bf16[16,128,16,128]{3,2,1,0:T(8,128)(2,1)} async-done(((bf16[16,128,16,128]{3,2,1,0:T(8,128)(2,1)}), bf16[16,128,16,128]{3,2,1,0:T(8,128)(2,1)}, u32[]{:S(2)}, u32[]{:S(2)}) %all-to-all-start) | async-done | bytes 8388640 | tf_op jit(solution)/shard_map/all_to_all | solution.py:76
  289.8 9.3 %copy.15 = bf16[128,16,16,128]{3,2,1,0:T(8,128)(2,1)} copy(bf16[128,16,16,128]{3,2,0,1:T(8,128)(2,1)} %bitcast.6) | data formatting | bytes 16777216 | tf_op jit(solution)/shard_map/reshape | solution.py:75
  299.1 11.1 %dynamic-slice_select_fusion.1 = (bf16[128,128,128]{2,1,0:T(8,128)(2,1)}, bf16[128,128,128]{2,1,0:T(8,128)(2,1)}) fusion(bf16[128,256,128]{2,1,0:T(8,128)(2,1)} %bitcast.42, s32[]{:T(128)S(6)} %select_n.63, pred[]{:T(512)S(6)} %eq.58, s32[]{:T(128)S(6)} %select_n.69, pred[]{:T(512)S(6)} %eq.61), kind=kLoop, calls=%fused_computation.10 | loop fusion | flops 4194304 | bytes 16777226 | tf_op jit(solution)/shard_map/jit(_where)/select_n | solution.py:12
  310.4 238.6 %all-reduce.4.cloned.1.call-done = (bf16[128,128,128]{2,1,0:T(8,128)(2,1)}, bf16[128,128,128]{2,1,0:T(8,128)(2,1)}) async-done(((bf16[128,128,128]{2,1,0:T(8,128)(2,1)}, bf16[128,128,128]{2,1,0:T(8,128)(2,1)}), (bf16[128,128,128]{2,1,0:T(8,128)(2,1)}, bf16[128,128,128]{2,1,0:T(8,128)(2,1)})) %all-reduce.4.cloned.1.call-update) | async-done | bytes 8388624 | tf_op jit(solution)/shard_map/psum | solution.py:13
  548.9 10.2 %convolution_convert_fusion.1 = bf16[128,128,256]{2,1,0:T(8,128)(2,1)} fusion(bf16[128,128,128]{2,1,0:T(8,128)(2,1)} %get-tuple-element.22, bf16[128,256,128]{2,1,0:T(8,128)(2,1)} %bitcast.43), kind=kOutput, calls=%fused_computation.6 | convolution fusion | flops 1077936128 | bytes 20971520 | tf_op jit(solution)/shard_map/mdt,mpt->mdp/dot_general | solution.py:56
  559.2 12.8 %copy.19 = bf16[16,8,128,256]{3,1,2,0:T(8,128)(2,1)} copy(bf16[16,8,128,256]{3,2,1,0:T(8,128)(2,1)} %bitcast.48) | data formatting | bytes 16777216
  572.0 11.9 %copy.16 = bf16[32768,128]{1,0:T(8,128)(2,1)} copy(bf16[32768,128]{0,1:T(8,128)(2,1)} %bitcast.49) | data formatting | bytes 16777216 | tf_op jit(solution)/shard_map/dot_general | solution.py:60
  583.9 10.2 %convolution_convert_fusion = bf16[128,128,256]{2,1,0:T(8,128)(2,1)} fusion(bf16[128,128,128]{2,1,0:T(8,128)(2,1)} %get-tuple-element.21, bf16[128,256,128]{2,1,0:T(8,128)(2,1)} %bitcast.44), kind=kOutput, calls=%fused_computation.5 | convolution fusion | flops 1077936128 | bytes 20971520 | tf_op jit(solution)/shard_map/mdt,mpt->mdp/dot_general | solution.py:56
  594.2 12.5 %copy.20 = bf16[16,8,128,256]{3,1,2,0:T(8,128)(2,1)} copy(bf16[16,8,128,256]{3,2,1,0:T(8,128)(2,1)} %bitcast.47) | data formatting | bytes 16777216
  606.7 11.5 %copy.17 = bf16[32768,128]{1,0:T(8,128)(2,1)} copy(bf16[32768,128]{0,1:T(8,128)(2,1)} %bitcast.50) | data formatting | bytes 16777216 | tf_op jit(solution)/shard_map/dot_general | solution.py:60
  618.2 9.0 %fusion = bf16[1,76,128,256]{3,1,2,0:T(8,128)(2,1)} fusion(pred[128,256]{1,0:T(8,128)(4,1)S(1)} %get-tuple-element.25, bf16[128,256,128]{2,1,0:T(8,128)(2,1)} %bitcast.45, f32[128]{0:T(128)S(1)} %get-tuple-element.36, f32[128]{0:T(128)S(1)} %get-tuple-element.35), kind=kOutput, calls=%fused_computation.7 | convolution fusion | flops 642563584 | bytes 13403136 | tf_op jit(solution)/shard_map/dot_general | solution.py:60
  627.2 5.5 fusion.1
  632.7 9.0 %pad_maximum_fusion = bf16[2,76,128,256]{3,1,2,0:T(8,128)(2,1)} fusion(bf16[1,76,128,256]{3,1,2,0:T(8,128)(2,1)} %fusion.1, bf16[1,76,128,256]{3,1,2,0:T(8,128)(2,1)} %fusion), kind=kLoop, calls=%fused_computation.2 | loop fusion | flops 4980736 | bytes 19922944 | tf_op jit(solution)/shard_map/stack | solution.py:91
  641.7 11.6 %copy.18 = bf16[2,76,128,256]{3,2,1,0:T(8,128)(2,1)} copy(bf16[2,76,128,256]{3,1,2,0:T(8,128)(2,1)} %pad_maximum_fusion) | data formatting | bytes 19922944 | tf_op jit(solution)/shard_map/stack | solution.py:91
  (208 shorter events, 85.2 us)
Async XLA Ops:
  101.2 9.1 %copy-start.1 = (s32[2,1]{0,1:T(1,128)S(1)}, s32[2,1]{0,1:T(1,128)}, u32[]{:S(2)}) copy-start(s32[2,1]{0,1:T(1,128)} %param.7) | copy-start | bytes 28
  101.2 188.6 %all-to-all-start = ((bf16[16,128,16,128]{3,2,1,0:T(8,128)(2,1)}), bf16[16,128,16,128]{3,2,1,0:T(8,128)(2,1)}, u32[]{:S(2)}, u32[]{:S(2)}) async-start(bf16[16,128,16,128]{3,2,1,0:T(8,128)(2,1)} %stack.12), calls=%async_computation | async-start | bytes 16777216 | tf_op jit(solution)/shard_map/all_to_all | solution.py:76
  110.0 438.9 %all-reduce.4.cloned.1.call-start = ((), (), s32[]{:S(2)}) async-start(), calls=%async_computation.1 | async-start | bytes 16777216 | tf_op jit(solution)/shard_map/psum | solution.py:13
  618.2 9.0 %copy-start = (bf16[32768,128]{1,0:T(8,128)(2,1)S(1)}, bf16[32768,128]{1,0:T(8,128)(2,1)}, u32[]{:S(2)}) copy-start(bf16[32768,128]{1,0:T(8,128)(2,1)} %copy.17) | copy-start | bytes 25165828
Sparse Core Ops, SparseCore 0:
  310.3 238.5 all-reduce.3
